TPU v7x, 32 devices: a whole 2x2x4 slice. The times are simulated.
32 devices in a mesh: grp: 2 (over y), band: 4 (over z), sect: 4 (over x, core).
Axes of the slice: x: 2, y: 2, z: 4, core: 2. Of those that a mesh axis runs over, the one named last changes fastest.
Arguments:
- features: bfloat16 [4, 24, 96, 2048], P('grp', 'band', None, 'sect'), parts along dimension 0, may hold values from -16 to 16
- low_level: bfloat16 [4, 24, 96, 256], P('grp', 'band'), parts along dimension 0, may hold values from -6 to 6
- land_mask: int32 [4, 24], P('grp', 'band'), parts along dimension 0, may hold values from 0 to 1, as said below
- weight_one: bfloat16 [2048, 256], P('sect'), may hold values from -0.125 to 0.125
- weight_dilated: bfloat16 [3, 3, 3, 2048, 256], P(None, None, None, 'sect'), may hold values from -0.046875 to 0.046875
- bias_branch: float32 [4, 256], replicated, may hold values from -3 to 3
- weight_pool: bfloat16 [2048, 256], P('sect'), may hold values from -0.125 to 0.125
- bias_pool: float32 [256], replicated, may hold values from -3 to 3
- weight_project: bfloat16 [1280, 256], replicated, may hold values from -0.15625 to 0.15625
- bias_project: float32 [256], replicated, may hold values from -3 to 3
- weight_reduce: bfloat16 [256, 48], replicated, may hold values from -0.375 to 0.375
- bias_reduce: float32 [48], replicated, may hold values from -3 to 3
- weight_merging: bfloat16 [3, 3, 304, 256], replicated, may hold values from -0.109375 to 0.109375
- bias_merging: float32 [256], replicated, may hold values from -3 to 3
Outputs:
- merged_map: bfloat16 [4, 24, 96, 256], P('grp', 'band'), parts along dimension 0
There are 2 independent parts, one for each index of `grp`. A program takes and returns all parts, laid end to end along the dimension named above; an argument that names none is the same for every part. Nothing has to cross between parts.
Inputs may be any that keep to these rules, and one draw needn't show every extreme that they name: `land_mask`: in every image each aligned block of 6 rows holds at most 4 ones and at least 2 ones, its first and last rows always being ones; in every image some block holds exactly 4.
All inputs are finite; a program needn't handle non-finite values.
Results may differ from a plain program's by a relative error of at most 0.012.
Values may be sent and summed in bfloat16 or wider, within the bound.
A program may use at most 64 MiB of HBM per device.

v0:
```python
import jax
import jax.numpy as jnp
from jax import lax
from jax.sharding import PartitionSpec as P

DILATIONS = (12, 24, 36)
PADDING = 36
PRECISE = lax.Precision.HIGHEST


def from_behind(value, axis, by):
    count = lax.axis_size(axis)
    pairs = [(i, i + by) for i in range(count) if 0 <= i + by < count]
    return lax.ppermute(value, axis, pairs)


def extended(block, sides, width):
    for axis, dim in sides:
        count = lax.axis_size(axis)
        forward = [(i, i + 1) for i in range(count - 1)]
        backward = [(target, source) for source, target in forward]
        low = lax.ppermute(
            lax.slice_in_dim(block, block.shape[dim] - width, None, axis=dim), axis, forward
        )
        high = lax.ppermute(lax.slice_in_dim(block, 0, width, axis=dim), axis, backward)
        block = jnp.concatenate([low, block, high], axis=dim)
    return block


def extend_rows(features):
    row_count = features.shape[1]
    reach_bands = min((PADDING + row_count - 1) // row_count, lax.axis_size("band") - 1)
    upper_blocks = []
    lower_blocks = []
    moving_up = features
    moving_down = features
    for hop_index in range(reach_bands):
        moving_up = from_behind(moving_up, "band", 1)
        moving_down = from_behind(moving_down, "band", -1)
        upper_blocks.insert(0, moving_up)
        lower_blocks.append(moving_down)
    margin = reach_bands * row_count
    stacked = jnp.concatenate(upper_blocks + [features] + lower_blocks, axis=1)
    if margin >= PADDING:
        stacked = stacked[:, margin - PADDING : margin + row_count + PADDING]
    else:
        stacked = jnp.pad(stacked, ((0, 0), (PADDING - margin, PADDING - margin), (0, 0), (0, 0)))
    return jnp.pad(stacked, ((0, 0), (0, 0), (PADDING, PADDING), (0, 0)))


def branch_terms(window, select_rows, weight_one, weight_dilated, live_rows, col_count):
    batches = window.shape[0]
    channels = window.shape[3]
    centre = select_rows(0)[:, :, PADDING : PADDING + col_count].reshape(-1, channels)
    partials = [jnp.dot(centre, weight_one, preferred_element_type=jnp.float32)]
    for branch_index, dilation in enumerate(DILATIONS):
        running = jnp.zeros((centre.shape[0], weight_one.shape[1]), jnp.float32)
        for row_tap in range(3):
            band_rows = select_rows(dilation * (row_tap - 1))
            for col_tap in range(3):
                left = PADDING + dilation * (col_tap - 1)
                tap_rows = band_rows[:, :, left : left + col_count].reshape(-1, channels)
                running = running + jnp.dot(
                    tap_rows,
                    weight_dilated[branch_index, row_tap, col_tap],
                    preferred_element_type=jnp.float32,
                )
        partials.append(running)
    return jnp.concatenate(partials, axis=1).reshape(batches, live_rows, col_count, -1)


def pool_context(features, weight_pool, bias_pool, row_count, col_count):
    local_sum = jnp.sum(features, axis=(1, 2), dtype=jnp.float32)
    cell_count = row_count * lax.axis_size("band") * col_count
    weight_full = weight_pool.astype(jnp.float32)
    average = lax.psum(local_sum, "band") / cell_count
    pre_relu = lax.psum(jnp.dot(average, weight_full, precision=PRECISE), "sect")
    return jax.nn.relu(pre_relu + bias_pool)


def shards(
    features,
    low_level,
    land_mask,
    weight_one,
    weight_dilated,
    bias_branch,
    weight_pool,
    bias_pool,
    weight_project,
    bias_project,
    weight_reduce,
    bias_reduce,
    weight_merging,
    bias_merging,
):
    batches, row_count, col_count, channels = features.shape
    branch_width = weight_project.shape[1]
    window = extend_rows(features)
    pooled = pool_context(features, weight_pool, bias_pool, row_count, col_count)
    context = jnp.dot(
        pooled, weight_project[4 * branch_width :].astype(jnp.float32), precision=PRECISE
    )
    row_mask = land_mask.astype(jnp.float32)

    def select_rows(offset):
        return window[:, PADDING + offset : PADDING + offset + row_count]

    partials = branch_terms(window, select_rows, weight_one, weight_dilated, row_count, col_count)
    flat_terms = partials.astype(jnp.bfloat16).reshape(-1, partials.shape[3])
    summed_cells = lax.psum_scatter(flat_terms, "sect", scatter_dimension=0, tiled=True).astype(
        jnp.float32
    )
    share_cells = summed_cells.shape[0]
    first_cell = lax.axis_index("sect") * share_cells
    branch_cells = jax.nn.relu(summed_cells + bias_branch.reshape(-1)).astype(jnp.bfloat16)
    projected_cells = jnp.dot(
        branch_cells, weight_project[: 4 * branch_width], preferred_element_type=jnp.float32
    )
    cell_ids = first_cell + lax.broadcasted_iota(jnp.int32, (share_cells,), 0)
    batch_of = cell_ids // (row_count * col_count)
    batch_onehot = (batch_of[:, None] == lax.broadcasted_iota(jnp.int32, (1, batches), 1)).astype(
        jnp.float32
    )
    context_cells = jnp.dot(batch_onehot, context, precision=PRECISE)
    keep_all = jnp.broadcast_to(row_mask[:, :, None], (batches, row_count, col_count)).reshape(-1)
    keep_cells = lax.dynamic_slice_in_dim(keep_all, first_cell, share_cells, 0)
    out_cells = (
        jax.nn.relu(projected_cells + context_cells + bias_project) * keep_cells[:, None]
    ).astype(jnp.bfloat16)
    project_out = lax.all_gather(out_cells, "sect", axis=0, tiled=True).reshape(
        batches, row_count, col_count, branch_width
    )
    low_reduced = (
        jax.nn.relu(
            jnp.dot(
                low_level.reshape(-1, low_level.shape[3]),
                weight_reduce,
                preferred_element_type=jnp.float32,
            )
            + bias_reduce
        )
        .astype(jnp.bfloat16)
        .reshape(batches, row_count, col_count, -1)
    )
    joined = jnp.concatenate([project_out, low_reduced], axis=3)
    framed = extended(joined, (("band", 1),), 1)
    framed = jnp.pad(framed, ((0, 0), (0, 0), (1, 1), (0, 0)))
    running = jnp.zeros((batches * row_count * col_count, weight_merging.shape[3]), jnp.float32)
    for row_tap in range(3):
        for col_tap in range(3):
            tap_rows = framed[
                :, row_tap : row_tap + row_count, col_tap : col_tap + col_count
            ].reshape(-1, joined.shape[3])
            running = running + jnp.dot(
                tap_rows, weight_merging[row_tap, col_tap], preferred_element_type=jnp.float32
            )
    merged_map = (
        jax.nn.relu(running + bias_merging).reshape(batches, row_count, col_count, -1)
        * row_mask[:, :, None, None]
    )
    return merged_map.astype(jnp.bfloat16)


def solution(mesh):
    in_specs = (
        P("grp", "band", None, "sect"),
        P("grp", "band", None, None),
        P("grp", "band"),
        P("sect", None),
        P(None, None, None, "sect", None),
        P(),
        P("sect", None),
        P(),
        P(),
        P(),
        P(),
        P(),
        P(),
        P(),
    )
    out_specs = P("grp", "band", None, None)
    return jax.shard_map(shards, mesh=mesh, in_specs=in_specs, out_specs=out_specs, check_vma=False)
```

profile of v0, /device:TPU:1, one launch (start us, length us, event | category | flops | bytes accessed | tf_op | source)
XLA Modules:
  0.0 204.5 jit_solution(5829789880484812974)
XLA Ops:
  6.5 4.2 %collective-permute-start = (bf16[2,6,96,512]{3,2,1,0:T(8,128)(2,1)}, bf16[2,6,96,512]{3,2,1,0:T(8,128)(2,1)S(1)}, u32[]{:S(2)}, u32[]{:S(2)}) collective-permute-start(bf16[2,6,96,512]{3,2,1,0:T(8,128)(2,1)} %param.14), channel_id=1, source_target_pairs={{0,4},{4,8},{8,12},{1,5},{5,9},{9,13},{2,6},{6,10},{10,14},{3,7},{... | collective-permute-start | bytes 3538952 | tf_op jit(solution)/shard_map/ppermute | solution.py:14
  10.8 1.3 collective-permute-start.3
  12.1 23.6 %collective-permute-done = bf16[2,6,96,512]{3,2,1,0:T(8,128)(2,1)S(1)} collective-permute-done((bf16[2,6,96,512]{3,2,1,0:T(8,128)(2,1)}, bf16[2,6,96,512]{3,2,1,0:T(8,128)(2,1)S(1)}, u32[]{:S(2)}, u32[]{:S(2)}) %collective-permute-start) | collective-permute-done | bytes 1179680 | tf_op jit(solution)/shard_map/ppermute | solution.py:14
  35.6 4.1 %collective-permute-start.1 = (bf16[2,6,96,512]{3,2,1,0:T(8,128)(2,1)S(1)}, bf16[2,6,96,512]{3,2,1,0:T(8,128)(2,1)S(1)}, u32[]{:S(2)}, u32[]{:S(2)}) collective-permute-start(bf16[2,6,96,512]{3,2,1,0:T(8,128)(2,1)S(1)} %collective-permute-done), channel_id=1, source_target_pairs={{0,4},{4,8},{8,12},{1,5},{5,9},{9,13},{2,6},{6,10},{10,14},{3,7},{... | collective-permute-start | bytes 3538952 | tf_op jit(solution)/shard_map/ppermute | solution.py:14
  39.7 2.4 %fusion.43 = f32[1152,256]{1,0:T(8,128)} fusion(bf16[3,3,3,512,256]{4,3,2,1,0:T(8,128)(2,1)} %param.18), kind=kOutput, calls=%fused_computation.92 | convolution fusion | flops 301989888 | bytes 1441792 | tf_op jit(solution)/shard_map/dot_general | solution.py:63
  42.2 2.5 %fusion.41 = f32[1152,256]{1,0:T(8,128)} fusion(bf16[3,3,3,512,256]{4,3,2,1,0:T(8,128)(2,1)} %param.18), kind=kOutput, calls=%fused_computation.90 | convolution fusion | flops 301989888 | bytes 1441792 | tf_op jit(solution)/shard_map/dot_general | solution.py:63
  44.7 1.3 convolution_convert_fusion
  46.0 1.5 collective-permute-start.4
  47.6 2.4 %fusion.39 = f32[1152,256]{1,0:T(8,128)} fusion(bf16[3,3,3,512,256]{4,3,2,1,0:T(8,128)(2,1)} %param.18), kind=kOutput, calls=%fused_computation.88 | convolution fusion | flops 301989888 | bytes 1441792 | tf_op jit(solution)/shard_map/dot_general | solution.py:63
  50.0 2.5 %fusion.78 = f32[1152,256]{1,0:T(8,128)} fusion(bf16[1152,512]{1,0:T(8,128)(2,1)S(1)} %bitcast.182, bf16[3,3,3,512,256]{4,3,2,1,0:T(8,128)(2,1)} %param.18), kind=kOutput, calls=%fused_computation.127 | convolution fusion | flops 301989888 | bytes 2621440 | tf_op jit(solution)/shard_map/dot_general | solution.py:63
  52.5 10.9 %collective-permute-done.1 = bf16[2,6,96,512]{3,2,1,0:T(8,128)(2,1)S(1)} collective-permute-done((bf16[2,6,96,512]{3,2,1,0:T(8,128)(2,1)S(1)}, bf16[2,6,96,512]{3,2,1,0:T(8,128)(2,1)S(1)}, u32[]{:S(2)}, u32[]{:S(2)}) %collective-permute-start.1) | collective-permute-done | bytes 1179680 | tf_op jit(solution)/shard_map/ppermute | solution.py:14
  63.4 4.2 %collective-permute-start.2 = (bf16[2,6,96,512]{3,2,1,0:T(8,128)(2,1)S(1)}, bf16[2,6,96,512]{3,2,1,0:T(8,128)(2,1)S(1)}, u32[]{:S(2)}, u32[]{:S(2)}) collective-permute-start(bf16[2,6,96,512]{3,2,1,0:T(8,128)(2,1)S(1)} %collective-permute-done.1), channel_id=1, source_target_pairs={{0,4},{4,8},{8,12},{1,5},{5,9},{9,13},{2,6},{6,10},{10,14},{3,7},{... | collective-permute-start | bytes 3538952 | tf_op jit(solution)/shard_map/ppermute | solution.py:14
  67.6 2.5 %fusion.37 = f32[1152,256]{1,0:T(8,128)} fusion(bf16[3,3,3,512,256]{4,3,2,1,0:T(8,128)(2,1)} %param.18), kind=kOutput, calls=%fused_computation.86 | convolution fusion | flops 301989888 | bytes 1441792 | tf_op jit(solution)/shard_map/dot_general | solution.py:63
  70.0 1.5 fusion.64
  71.6 1.5 fusion.51
  73.9 1.3 collective-permute-start.5
  75.2 1.5 fusion.84
  76.6 1.6 fusion.73
  78.2 12.2 %collective-permute-done.2 = bf16[2,6,96,512]{3,2,1,0:T(8,128)(2,1)S(1)} collective-permute-done((bf16[2,6,96,512]{3,2,1,0:T(8,128)(2,1)S(1)}, bf16[2,6,96,512]{3,2,1,0:T(8,128)(2,1)S(1)}, u32[]{:S(2)}, u32[]{:S(2)}) %collective-permute-start.2) | collective-permute-done | bytes 1179680 | tf_op jit(solution)/shard_map/ppermute | solution.py:14
  90.9 9.7 %collective-permute-done.5 = bf16[2,6,96,512]{3,2,1,0:T(8,128)(2,1)S(1)} collective-permute-done((bf16[2,6,96,512]{3,2,1,0:T(8,128)(2,1)S(1)}, bf16[2,6,96,512]{3,2,1,0:T(8,128)(2,1)S(1)}, u32[]{:S(2)}, u32[]{:S(2)}) %collective-permute-start.5) | collective-permute-done | bytes 1179680 | tf_op jit(solution)/shard_map/ppermute | solution.py:14
  100.7 12.3 %pad_slice_fusion.11 = (bf16[2,6,96,512]{3,2,1,0:T(8,128)(2,1)S(1)}, bf16[2,6,96,512]{3,2,1,0:T(8,128)(2,1)S(1)}, bf16[2,6,96,512]{3,2,1,0:T(8,128)(2,1)}, bf16[...) fusion(bf16[2,42,96,512]{3,2,1,0:T(8,128)(2,1)S(1)} %constant_d, ...), kind=kLoop, calls=%fused_computation.11 | loop fusion | bytes 29491200 | tf_op jit(solution)/shard_map/slice | solution.py:62
  113.0 1.8 fusion.80
  132.8 1.8 pad_maximum_fusion
  135.7 7.8 %psum.14 = f32[2,512]{1,0:T(2,128)S(1)} all-reduce(f32[2,512]{1,0:T(2,128)S(1)} %convert_reduce_fusion), channel_id=1, replica_groups=mesh['grp'=2,'band'=4,'sect'=4] {'band'}, use_global_device_ids=true, to_apply=%region_2.3 | all-reduce | flops 1024 | bytes 8192 | tf_op jit(solution)/shard_map/psum | solution.py:76
  143.7 10.6 %psum.15 = f32[2,256]{1,0:T(2,128)S(1)} all-reduce(f32[2,256]{1,0:T(2,128)S(1)} %fusion.137), channel_id=1, replica_groups=mesh['grp'=2,'band'=4,'sect'=4] {'sect'}, use_global_device_ids=true, to_apply=%region_3.4 | all-reduce | flops 512 | bytes 4096 | tf_op jit(solution)/shard_map/psum | solution.py:77
  154.9 15.6 %reduce-scatter.2.cloned.1.call-done = bf16[288,1024]{1,0:T(8,128)(2,1)} async-done(((bf16[1152,1024]{1,0:T(8,128)(2,1)}), bf16[288,1024]{1,0:T(8,128)(2,1)}) %reduce-scatter.2.cloned.1.call-update) | async-done | bytes 589840 | tf_op jit(solution)/shard_map/reduce_scatter | solution.py:111
  170.5 1.4 fusion.34
  172.2 7.9 %all_gather.3 = bf16[1152,256]{1,0:T(8,128)(2,1)S(1)} all-gather(bf16[288,256]{1,0:T(8,128)(2,1)S(1)} %fusion.30), channel_id=1, replica_groups=mesh['grp'=2,'band'=4,'sect'=4] {'sect'}, dimensions={0}, use_global_device_ids=true | all-gather | bytes 737280 | tf_op jit(solution)/shard_map/all_gather | solution.py:131
  180.1 3.1 %collective-permute-start.6 = (bf16[2,1,96,304]{3,2,1,0:T(8,128)(2,1)S(1)}, bf16[2,1,96,304]{3,2,1,0:T(8,128)(2,1)S(1)}, u32[]{:S(2)}, u32[]{:S(2)}) collective-permute-start(bf16[2,1,96,304]{3,2,1,0:T(8,128)(2,1)S(1)} %get-tuple-element.31), channel_id=1, source_target_pairs={{0,4},{4,8},{8,12},{1,5},{5,9},{9,13},{2,6},{6,10},{10,14},{3,7},{... | collective-permute-start | bytes 350216 | tf_op jit(solution)/shard_map/ppermute | solution.py:22
  183.2 1.3 collective-permute-start.7
  184.5 1.7 collective-permute-done.6
  186.2 3.8 %collective-permute-done.7 = bf16[2,1,96,304]{3,2,1,0:T(8,128)(2,1)S(1)} collective-permute-done((bf16[2,1,96,304]{3,2,1,0:T(8,128)(2,1)S(1)}, bf16[2,1,96,304]{3,2,1,0:T(8,128)(2,1)S(1)}, u32[]{:S(2)}, u32[]{:S(2)}) %collective-permute-start.7) | collective-permute-done | bytes 116768 | tf_op jit(solution)/shard_map/ppermute | solution.py:25
  (115 shorter events, 28.6 us)
Async XLA Ops:
  6.5 148.0 %copy-start = (bf16[2,6,96,256]{3,2,1,0:T(8,128)(2,1)S(1)}, bf16[2,6,96,256]{3,2,1,0:T(8,128)(2,1)}, u32[]{:S(2)}) copy-start(bf16[2,6,96,256]{3,2,1,0:T(8,128)(2,1)} %param.15) | copy-start | bytes 1769476
  6.5 163.9 %reduce-scatter.2.cloned.1.call-start = ((), (), s32[]{:S(2)}) async-start(), calls=%async_computation.1 | async-start | bytes 2949120 | tf_op jit(solution)/shard_map/reduce_scatter | solution.py:111
  6.5 29.1 %collective-permute-start = (bf16[2,6,96,512]{3,2,1,0:T(8,128)(2,1)}, bf16[2,6,96,512]{3,2,1,0:T(8,128)(2,1)S(1)}, u32[]{:S(2)}, u32[]{:S(2)}) collective-permute-start(bf16[2,6,96,512]{3,2,1,0:T(8,128)(2,1)} %param.14), channel_id=1, source_target_pairs={{0,4},{4,8},{8,12},{1,5},{5,9},{9,13},{2,6},{6,10},{10,14},{3,7},{... | collective-permute-start | bytes 3538952 | tf_op jit(solution)/shard_map/ppermute | solution.py:14
  10.8 35.2 %collective-permute-start.3 = (bf16[2,6,96,512]{3,2,1,0:T(8,128)(2,1)}, bf16[2,6,96,512]{3,2,1,0:T(8,128)(2,1)S(1)}, u32[]{:S(2)}, u32[]{:S(2)}) collective-permute-start(bf16[2,6,96,512]{3,2,1,0:T(8,128)(2,1)} %param.14), channel_id=1, source_target_pairs={{4,0},{8,4},{12,8},{5,1},{9,5},{13,9},{6,2},{10,6},{14,10},{7,3},{... | collective-permute-start | bytes 3538952 | tf_op jit(solution)/shard_map/ppermute | solution.py:14
  35.6 27.8 %collective-permute-start.1 = (bf16[2,6,96,512]{3,2,1,0:T(8,128)(2,1)S(1)}, bf16[2,6,96,512]{3,2,1,0:T(8,128)(2,1)S(1)}, u32[]{:S(2)}, u32[]{:S(2)}) collective-permute-start(bf16[2,6,96,512]{3,2,1,0:T(8,128)(2,1)S(1)} %collective-permute-done), channel_id=1, source_target_pairs={{0,4},{4,8},{8,12},{1,5},{5,9},{9,13},{2,6},{6,10},{10,14},{3,7},{... | collective-permute-start | bytes 3538952 | tf_op jit(solution)/shard_map/ppermute | solution.py:14
  42.1 2.6 %copy-start.1 = (bf16[2,6,96,512]{3,2,1,0:T(8,128)(2,1)S(1)}, bf16[2,6,96,512]{3,2,1,0:T(8,128)(2,1)}, u32[]{:S(2)}) copy-start(bf16[2,6,96,512]{3,2,1,0:T(8,128)(2,1)} %param.14) | copy-start | bytes 3538948
  42.1 2.6 %copy-start.22 = (bf16[512,256]{1,0:T(8,128)(2,1)S(1)}, bf16[512,256]{1,0:T(8,128)(2,1)}, u32[]{:S(2)}) copy-start(bf16[512,256]{1,0:T(8,128)(2,1)} %param.17) | copy-start | bytes 786436
  44.7 25.3 %copy-start.2 = (bf16[3,3,3,512,256]{4,3,2,1,0:T(8,128)(2,1)S(1)}, bf16[3,3,3,512,256]{4,3,2,1,0:T(8,128)(2,1)}, u32[]{:S(2)}) copy-start(bf16[3,3,3,512,256]{4,3,2,1,0:T(8,128)(2,1)} %param.18) | copy-start | bytes 21233668
  46.0 27.9 %collective-permute-start.4 = (bf16[2,6,96,512]{3,2,1,0:T(8,128)(2,1)S(1)}, bf16[2,6,96,512]{3,2,1,0:T(8,128)(2,1)S(1)}, u32[]{:S(2)}, u32[]{:S(2)}) collective-permute-start(bf16[2,6,96,512]{3,2,1,0:T(8,128)(2,1)S(1)} %collective-permute-done.3), channel_id=1, source_target_pairs={{4,0},{8,4},{12,8},{5,1},{9,5},{13,9},{6,2},{10,6},{14,10},{7,3},{... | collective-permute-start | bytes 3538952 | tf_op jit(solution)/shard_map/ppermute | solution.py:14
  63.4 27.0 %collective-permute-start.2 = (bf16[2,6,96,512]{3,2,1,0:T(8,128)(2,1)S(1)}, bf16[2,6,96,512]{3,2,1,0:T(8,128)(2,1)S(1)}, u32[]{:S(2)}, u32[]{:S(2)}) collective-permute-start(bf16[2,6,96,512]{3,2,1,0:T(8,128)(2,1)S(1)} %collective-permute-done.1), channel_id=1, source_target_pairs={{0,4},{4,8},{8,12},{1,5},{5,9},{9,13},{2,6},{6,10},{10,14},{3,7},{... | collective-permute-start | bytes 3538952 | tf_op jit(solution)/shard_map/ppermute | solution.py:14
  73.9 26.7 %collective-permute-start.5 = (bf16[2,6,96,512]{3,2,1,0:T(8,128)(2,1)S(1)}, bf16[2,6,96,512]{3,2,1,0:T(8,128)(2,1)S(1)}, u32[]{:S(2)}, u32[]{:S(2)}) collective-permute-start(bf16[2,6,96,512]{3,2,1,0:T(8,128)(2,1)S(1)} %collective-permute-done.4), channel_id=1, source_target_pairs={{4,0},{8,4},{12,8},{5,1},{9,5},{13,9},{6,2},{10,6},{14,10},{7,3},{... | collective-permute-start | bytes 3538952 | tf_op jit(solution)/shard_map/ppermute | solution.py:14
  113.0 1.8 copy-start.6
  114.9 1.3 copy-start.5
  120.6 1.3 copy-start.12
  120.6 1.6 copy-start.13
  122.2 1.3 copy-start.9
  122.2 1.6 copy-start.14
  124.3 1.3 copy-start.11
  124.3 1.6 copy-start.18
  125.9 1.6 copy-start.19
  128.0 1.3 copy-start.10
  128.1 1.6 copy-start.17
  129.7 1.6 copy-start.20
  134.6 8.9 %copy-start.21 = (bf16[512,256]{1,0:T(8,128)(2,1)S(1)}, bf16[512,256]{1,0:T(8,128)(2,1)}, u32[]{:S(2)}) copy-start(bf16[512,256]{1,0:T(8,128)(2,1)} %param.20) | copy-start | bytes 786436
  134.6 19.7 %copy-start.23 = (bf16[1280,256]{1,0:T(8,128)(2,1)S(1)}, bf16[1280,256]{1,0:T(8,128)(2,1)}, u32[]{:S(2)}) copy-start(bf16[1280,256]{1,0:T(8,128)(2,1)} %param.22) | copy-start | bytes 1966084
  134.7 19.7 %copy-start.25 = (f32[256]{0:T(256)S(1)}, f32[256]{0:T(256)}, u32[]{:S(2)}) copy-start(f32[256]{0:T(256)} %param.21) | copy-start | bytes 3076
  134.7 19.9 %copy-start.29 = (bf16[256,48]{0,1:T(8,128)(2,1)S(1)}, bf16[256,48]{0,1:T(8,128)(2,1)}, u32[]{:S(2)}) copy-start(bf16[256,48]{0,1:T(8,128)(2,1)} %param.24) | copy-start | bytes 73732
  134.7 19.9 %copy-start.30 = (f32[48]{0:T(128)S(1)}, f32[48]{0:T(128)}, u32[]{:S(2)}) copy-start(f32[48]{0:T(128)} %param.25) | copy-start | bytes 580
  154.9 17.0 %copy-start.26 = (f32[256]{0:T(256)S(1)}, f32[256]{0:T(256)}, u32[]{:S(2)}) copy-start(f32[256]{0:T(256)} %param.23) | copy-start | bytes 3076
  180.1 6.1 %collective-permute-start.6 = (bf16[2,1,96,304]{3,2,1,0:T(8,128)(2,1)S(1)}, bf16[2,1,96,304]{3,2,1,0:T(8,128)(2,1)S(1)}, u32[]{:S(2)}, u32[]{:S(2)}) collective-permute-start(bf16[2,1,96,304]{3,2,1,0:T(8,128)(2,1)S(1)} %get-tuple-element.31), channel_id=1, source_target_pairs={{0,4},{4,8},{8,12},{1,5},{5,9},{9,13},{2,6},{6,10},{10,14},{3,7},{... | collective-permute-start | bytes 350216 | tf_op jit(solution)/shard_map/ppermute | solution.py:22
  183.2 6.9 %collective-permute-start.7 = (bf16[2,1,96,304]{3,2,1,0:T(8,128)(2,1)S(1)}, bf16[2,1,96,304]{3,2,1,0:T(8,128)(2,1)S(1)}, u32[]{:S(2)}, u32[]{:S(2)}) collective-permute-start(bf16[2,1,96,304]{3,2,1,0:T(8,128)(2,1)S(1)} %get-tuple-element.32), channel_id=1, source_target_pairs={{4,0},{8,4},{12,8},{5,1},{9,5},{13,9},{6,2},{10,6},{14,10},{7,3},{... | collective-permute-start | bytes 350216 | tf_op jit(solution)/shard_map/ppermute | solution.py:25
  190.6 1.4 copy-start.16
  (8 other events, 8.2 us)
Sparse Core Ops, SparseCore 0:
  134.7 35.6 reduce-scatter.1
where the time goes:
time: 207 us; the launch traced here: 204 us
  waiting for transfers between devices  78.3 us (38%)
  matrix products  36.1 us (17%)
  blocking collectives  26.3 us (13%)
  local copies, waits for them, and re-layouts  25.2 us (12%)
  starting transfers between devices  21 us (10%)
  between operations  14 us (7%)
  other arithmetic  3.7 us (2%)
    ppermute x6, waiting for transfers between devices, from_behind(): return lax.ppermute(value, axis, pairs)  57.1 us
    dot_general x27, matrix products, branch_terms(): jnp.dot(tap_rows, weight_dilated[branch_index, row_tap, col_tap], preferr...  28.3 us
    ppermute x6, starting transfers between devices, from_behind(): return lax.ppermute(value, axis, pairs)  16.6 us
    reduce_scatter x1, waiting for transfers between devices, shards(): lax.psum_scatter(flat_terms, 'sect', scatter_dimension=0, tiled=True)  15.6 us
    slice x1, local copies, waits for them, and re-layouts, branch_terms(): tap_rows = band_rows[:, :, left:left + col_count].reshape(-1, channels)  12.3 us
    unnamed x69, local copies, waits for them, and re-layouts  11.7 us
    psum x1, blocking collectives, pool_context(): lax.psum(jnp.dot(average, weight_full, precision=PRECISE), 'sect')  10.6 us
    all_gather x1, blocking collectives, shards(): lax.all_gather(out_cells, 'sect', axis=0, tiled=True)  7.86 us
  transfers between devices with their start and end apart: 9, of which 8 were waited for; matrix products, arithmetic and copies ran while one was open for 10% of the time, Pallas kernels for 0%

commit v1 on v0

v1 whole, which is shorter than its diff:
```python
import functools

import jax
import jax.numpy as jnp
from jax import lax
from jax.experimental import pallas as pl
from jax.experimental.pallas import tpu as pltpu
from jax.sharding import PartitionSpec as P

DILATIONS = (12, 24, 36)
LAND_BLOCK = 6
LAND_MOST = 4
PRECISE = lax.Precision.HIGHEST
MESH = pl.DeviceIdType.MESH
F32 = jnp.float32
BF16 = jnp.bfloat16


def plan(rows, bands):
    off = []
    for k in (1, 2, 3):
        d = DILATIONS[k - 1]
        assert d % rows == 0
        hop = d // rows
        if hop < bands:
            off.append((k, 0, hop))
            off.append((k, 2, hop))
    order = [k for k in (3, 2, 1, 0)]
    return off, order


def kernel(
    dims, mask, feat_h, low_h, w1_h, wd_h, bbr, wpool_h, bpool, wproj_h, bproj, wr, br, wm_h, bm,
    out,
    feat, low, low_halo, w1, wd, wpool, wproj, wm, comp, m_l, m_r,
    part_off, crecv_off, xsend_off, xrecv_off, zsend, zrecv,
    part_own, crecv_own, xsend_own, xrecv_own, keep_off, keep_own,
    sums, pool_s, pool_b, gath, halo, joined, lowred, lowacc, outc,
    loc_sem, lo_s, lo_r, c_s, c_r, x_s, x_r, z_s, z_r, ps_s, ps_r, pb_s, pb_r,
    g_s, g_r, h_s, h_r,
):
    mb, rows, cols, ch, br_w, live, nb, ns, low_w, lowp = dims
    nx = ns // 2
    cs = cols // nx
    off, order = plan(rows, nb)
    n_off = len(off)
    need = [(k, 1) for k in order if k] + [(k, i) for k, i, _ in off]
    pad = (m_l.shape[1] - cols) // 2

    band = lax.axis_index("band")
    sect = lax.axis_index("sect")
    core = lax.rem(sect, 2)
    xi = lax.div(sect, 2)

    locals_ = {}

    def fetch(name, src, dst):
        c = pltpu.make_async_copy(src, dst, loc_sem.at[len(locals_)])
        locals_[name] = c
        c.start()

    fetch("feat", feat_h, feat)
    for k, i, _ in off:
        fetch((k, i), wd_h.at[k - 1, i], wd.at[need.index((k, i))])
    for k in order:
        if k:
            fetch((k, 1), wd_h.at[k - 1, 1], wd.at[need.index((k, 1))])
        else:
            fetch("w1", w1_h, w1)
    fetch("wpool", wpool_h, wpool)
    fetch("low", low_h, low)
    fetch("wproj", wproj_h, wproj)
    fetch("wm", wm_h, wm)

    bar = pltpu.get_barrier_semaphore()
    up_ok = band >= 1
    dn_ok = band + 1 < nb

    def hello(b, s):
        pl.semaphore_signal(bar, inc=1, device_id={"band": b, "sect": s}, device_id_type=MESH)

    for e in range(1, ns):
        hello(band, lax.rem(sect + e, ns))
    for e in range(1, nb):
        hello(lax.rem(band + e, nb), sect)
    for ok, step in ((up_ok, -1), (dn_ok, 1)):
        @pl.when(ok)
        def _(step=step):
            for e in range(1, ns):
                hello(band + step, lax.rem(sect + e, ns))
    sides_held = jnp.minimum(band, 1) + jnp.minimum(nb - 1 - band, 1)
    pl.semaphore_wait(bar, (ns - 1) + (nb - 1) + (ns - 1) * sides_held)

    def rcopy(src, dst, s, r, **where):
        return pltpu.make_async_remote_copy(
            src_ref=src, dst_ref=dst, send_sem=s, recv_sem=r, device_id=where, device_id_type=MESH
        )

    low_up = rcopy(low_h.at[:, 0], low_halo.at[1], lo_s.at[0], lo_r.at[1], band=band - 1, sect=sect)
    low_dn = rcopy(
        low_h.at[:, rows - 1], low_halo.at[0], lo_s.at[1], lo_r.at[0], band=band + 1, sect=sect
    )

    @pl.when(up_ok)
    def _():
        low_up.start()

    @pl.when(dn_ok)
    def _():
        low_dn.start()

    def slots(m):
        on = [mask[m, y] for y in range(rows)]
        slot_of = [jnp.int32(0)] + [None] * (rows - 2) + [jnp.int32(live - 1)]
        row_of = [jnp.int32(0)] * live
        row_of[live - 1] = jnp.int32(rows - 1)
        held = [jnp.int32(0)] * live
        held[0] = on[0]
        held[live - 1] = on[rows - 1]
        count = jnp.int32(0)
        for y in range(1, rows - 1):
            slot_of[y] = jnp.where(on[y] > 0, jnp.minimum(count + 1, live - 1), 0)
            for r in range(1, live - 1):
                hit = jnp.logical_and(on[y] > 0, count == r - 1)
                row_of[r] = jnp.where(hit, y, row_of[r])
                held[r] = jnp.where(hit, 1, held[r])
            count = count + on[y]
        return on, slot_of, row_of, held

    for ref in (m_l, m_r):
        zero = jnp.zeros((ref.shape[0], pad, br_w), F32)
        ref[:, :pad] = zero
        ref[:, pad + cols :] = zero

    locals_["feat"].wait()

    def taps(lhs, n, wref, d):
        mid = jnp.dot(lhs, wref[1], preferred_element_type=F32).reshape(n, cols, br_w)
        m_l[:n, pl.ds(pad, cols)] = jnp.dot(
            lhs, wref[0], preferred_element_type=F32
        ).reshape(n, cols, br_w)
        m_r[:n, pl.ds(pad, cols)] = jnp.dot(
            lhs, wref[2], preferred_element_type=F32
        ).reshape(n, cols, br_w)
        return mid + m_l[:n, pl.ds(pad - d, cols)] + m_r[:n, pl.ds(pad + d, cols)]

    def core_copy(t):
        if t < n_off:
            src, dst = part_off.at[t, 0], crecv_off.at[t]
        else:
            src, dst = part_own.at[t - n_off, 0], crecv_own.at[t - n_off]
        return rcopy(src, dst, c_s.at[t], c_r.at[t], sect=xi * 2 + 1 - core)

    def x_copy(t, e, incoming=False):
        send, recv, u = (
            (xsend_off, xrecv_off, t) if t < n_off else (xsend_own, xrecv_own, t - n_off)
        )
        other = lax.rem(xi + e, nx)
        slot = other if incoming else xi
        return rcopy(
            send.at[u, other], recv.at[u, slot], x_s.at[t, other], x_r.at[t, slot],
            sect=other * 2 + core,
        )

    def first(t):
        def body(step, carry):
            image = jnp.where(step == 0, 1 - core, core)
            if t < n_off:
                k, i, _ = off[t]
                lhs = feat[image].reshape(rows * cols, ch)
                val = taps(lhs, rows, wd.at[need.index((k, i))], DILATIONS[k - 1])
                part_off[t, step] = val.astype(BF16)
            else:
                k = order[t - n_off]
                lhs = comp[image].reshape(live * cols, ch)
                if k:
                    val = taps(lhs, live, wd.at[need.index((k, 1))], DILATIONS[k - 1])
                else:
                    val = jnp.dot(lhs, w1[...], preferred_element_type=F32).reshape(
                        live, cols, br_w
                    )
                part_own[t - n_off, step] = val.astype(BF16)

            @pl.when(step == 0)
            def _():
                core_copy(t).start()
            return carry

        lax.fori_loop(0, 2, body, 0)

    def second(t):
        core_copy(t).wait_recv()
        part, got, send, keep, u = (
            (part_off, crecv_off, xsend_off, keep_off, t)
            if t < n_off
            else (part_own, crecv_own, xsend_own, keep_own, t - n_off)
        )
        for c in range(nx):
            cell = pl.ds(c * cs, cs)
            total = part[u, 1, :, cell].astype(F32) + got[u, :, cell].astype(F32)
            send[u, c] = total.astype(BF16)

            @pl.when(xi == c)
            def _():
                keep[u] = total
        for e in range(1, nx):
            x_copy(t, e).start()

    def shared(t):
        recv, keep, u = (
            (xrecv_off, keep_off, t) if t < n_off else (xrecv_own, keep_own, t - n_off)
        )
        total = keep[u]
        for e in range(1, nx):
            x_copy(t, e, True).wait_recv()
            total = total + recv[u, lax.rem(xi + e, nx)].astype(F32)
        return total

    def sends_to(t):
        k, i, hop = off[t]
        return band + hop < nb if i == 0 else band - hop >= 0

    def gets_from(t):
        k, i, hop = off[t]
        return band - hop >= 0 if i == 0 else band + hop < nb

    def z_copy(t):
        k, i, hop = off[t]
        return rcopy(
            zsend.at[t], zrecv.at[t], z_s.at[t], z_r.at[t],
            band=band + hop if i == 0 else band - hop, sect=sect,
        )

    def third_off(t):
        zsend[t] = shared(t).astype(BF16)
        z_copy(t).start()

    def guarded(fn, t):
        @pl.when(sends_to(t))
        def _():
            fn(t)

    for t in range(n_off):
        locals_[off[t][:2]].wait()
        guarded(first, t)

    facts = [slots(m) for m in range(mb)]
    sums[...] = jnp.zeros_like(sums)
    for m in range(mb):
        for r in range(live):
            comp[m, r] = feat[m, facts[m][2][r]]

    t0 = n_off
    locals_[(order[0], 1) if order[0] else "w1"].wait()
    first(t0)
    for t in range(n_off):
        guarded(second, t)

    locals_["wpool"].wait()
    for m in range(mb):
        acc = jnp.zeros((cols, ch), F32)
        for y in range(rows):
            acc = acc + feat[m, y].astype(F32)
        sums[m : m + 1, :] = jnp.sum(acc, axis=0, keepdims=True)
    pool_s[sect] = jnp.dot(
        sums[...], wpool[...].astype(F32), precision=PRECISE, preferred_element_type=F32
    )

    def pool_sect(e, incoming=False):
        other = lax.rem(sect + e, ns)
        slot = other if incoming else sect
        return rcopy(
            pool_s.at[sect], pool_s.at[slot], ps_s.at[other], ps_r.at[slot], sect=other
        )

    def pool_band(e, incoming=False):
        other = lax.rem(band + e, nb)
        slot = other if incoming else band
        return rcopy(
            pool_b.at[band], pool_b.at[slot], pb_s.at[other], pb_r.at[slot], band=other
        )

    for e in range(1, ns):
        pool_sect(e).start()

    locals_[(order[1], 1) if order[1] else "w1"].wait()
    first(t0 + 1)
    second(t0)
    for t in range(n_off):
        guarded(third_off, t)

    for e in range(1, ns):
        pool_sect(e, True).wait_recv()
    total = pool_s[0]
    for s in range(1, ns):
        total = total + pool_s[s]
    pool_b[band] = total
    for e in range(1, nb):
        pool_band(e).start()

    for u in (2, 3):
        locals_[(order[u], 1) if order[u] else "w1"].wait()
        first(t0 + u)
        second(t0 + u - 1)
    second(t0 + 3)

    locals_["low"].wait()
    locals_["wm"].wait()

    def reduced(v):
        return jax.nn.relu(
            jnp.dot(v, wr[...], preferred_element_type=F32) + br[...]
        ).astype(BF16)

    for m in range(mb):
        lowred[m, 1 : rows + 1] = reduced(low[m].reshape(rows * cols, low_w)).reshape(
            rows, cols, lowp
        )
    for side, at, ok, copy in ((0, 0, up_ok, low_dn), (1, rows + 1, dn_ok, low_up)):
        @pl.when(ok)
        def _(side=side, at=at, copy=copy):
            copy.wait_recv()
            for m in range(mb):
                lowred[m, at] = reduced(low_halo[side, m])

        @pl.when(jnp.logical_not(ok))
        def _(at=at):
            for m in range(mb):
                lowred[m, at] = jnp.zeros((cols, lowp), BF16)

    def merged(source, m, lo, n):
        row_of = facts[m][2]
        sides = [None] * 3
        for i in range(3):
            lhs = jnp.concatenate([source[m, row_of[r] + i] for r in range(live)], axis=0)
            for j in range(3):
                term = jnp.dot(
                    lhs, wm[i, j, lo : lo + n], preferred_element_type=F32
                )
                sides[j] = term if sides[j] is None else sides[j] + term
        m_l[:live, pl.ds(pad, cols)] = sides[0].reshape(live, cols, br_w)
        m_r[:live, pl.ds(pad, cols)] = sides[2].reshape(live, cols, br_w)
        return (
            sides[1].reshape(live, cols, br_w)
            + m_l[:live, pl.ds(pad - 1, cols)]
            + m_r[:live, pl.ds(pad + 1, cols)]
        )

    for m in range(mb):
        lowacc[m] = merged(lowred, m, br_w, lowp) + bm[...].reshape(1, 1, br_w)

    locals_["wproj"].wait()
    for e in range(1, nb):
        pool_band(e, True).wait_recv()
    total = pool_b[0]
    for b in range(1, nb):
        total = total + pool_b[b]
    pooled = jax.nn.relu(total / (nb * rows * cols) + bpool[...])
    context = jnp.dot(
        pooled, wproj[4 * br_w :].astype(F32), precision=PRECISE, preferred_element_type=F32
    )
    mine = context[0:1]
    for m in range(1, mb):
        mine = jnp.where(core == m, context[m : m + 1], mine)
    base = mine + bproj[...]

    _, _, own_row, own_held = slots(core)
    acc = jnp.zeros((live * cs, br_w), F32)
    for u, k in enumerate(order):
        keep_own[u] = shared(t0 + u)
        for t in range(n_off):
            if off[t][0] == k:
                @pl.when(gets_from(t))
                def _(t=t, u=u):
                    z_copy(t).wait_recv()
                    for r in range(live):
                        keep_own[u, r] = keep_own[u, r] + zrecv[t, own_row[r]].astype(F32)
        branch = jax.nn.relu(keep_own[u] + bbr[k : k + 1].reshape(1, 1, br_w)).astype(BF16)
        acc = acc + jnp.dot(
            branch.reshape(live * cs, br_w), wproj[k * br_w : (k + 1) * br_w],
            preferred_element_type=F32,
        )
    done = jax.nn.relu(acc + base).reshape(live, cs, br_w)
    for r in range(live):
        gath[sect, r] = (done[r] * own_held[r].astype(F32)).astype(BF16)

    def gather_copy(e, incoming=False):
        other = lax.rem(sect + e, ns)
        slot = other if incoming else sect
        return rcopy(gath.at[sect], gath.at[slot], g_s.at[other], g_r.at[slot], sect=other)

    def halo_copy(side, e, incoming=False):
        other = lax.rem(sect + e, ns)
        slot = other if incoming else sect
        src = gath.at[sect, live - 1 if side == 0 else 0]
        return rcopy(
            src, halo.at[side, slot], h_s.at[side, other], h_r.at[side, slot],
            band=band + 1 if side == 0 else band - 1, sect=other,
        )

    for e in range(1, ns):
        gather_copy(e).start()
    for side, ok in ((0, dn_ok), (1, up_ok)):
        @pl.when(ok)
        def _(side=side):
            for e in range(ns):
                halo_copy(side, e).start()
    for e in range(1, ns):
        gather_copy(e, True).wait_recv()
    for m in range(mb):
        on, slot_of, _, _ = facts[m]
        for y in range(rows):
            for c in range(nx):
                joined[m, y + 1, pl.ds(c * cs, cs)] = (
                    gath[c * 2 + m, slot_of[y]].astype(F32) * on[y].astype(F32)
                ).astype(BF16)
    for side, at, ok in ((0, 0, up_ok), (1, rows + 1, dn_ok)):
        @pl.when(ok)
        def _(side=side, at=at):
            for e in range(ns):
                halo_copy(side, e, True).wait_recv()
            for m in range(mb):
                for c in range(nx):
                    joined[m, at, pl.ds(c * cs, cs)] = halo[side, c * 2 + m]

        @pl.when(jnp.logical_not(ok))
        def _(at=at):
            for m in range(mb):
                joined[m, at] = jnp.zeros((cols, br_w), BF16)

    for m in range(mb):
        on, slot_of, _, _ = facts[m]
        outc[...] = jax.nn.relu(merged(joined, m, 0, br_w) + lowacc[m])
        for y in range(rows):
            out[m, y] = (outc[slot_of[y]] * on[y].astype(F32)).astype(BF16)

    @pl.when(up_ok)
    def _():
        low_up.wait_send()

    @pl.when(dn_ok)
    def _():
        low_dn.wait_send()

    def left(t):
        core_copy(t).wait_send()
        for e in range(1, nx):
            x_copy(t, e).wait_send()

    for t in range(n_off):
        guarded(left, t)
        guarded(lambda t: z_copy(t).wait_send(), t)
    for u in range(4):
        left(t0 + u)
    for e in range(1, ns):
        pool_sect(e).wait_send()
        gather_copy(e).wait_send()
    for e in range(1, nb):
        pool_band(e).wait_send()
    for side, ok in ((0, dn_ok), (1, up_ok)):
        @pl.when(ok)
        def _(side=side):
            for e in range(ns):
                halo_copy(side, e).wait_send()


def shards(
    features, low_level, land_mask, weight_one, weight_dilated, bias_branch, weight_pool,
    bias_pool, weight_project, bias_project, weight_reduce, bias_reduce, weight_merging,
    bias_merging,
):
    mb, rows, cols, ch = features.shape
    br_w = weight_project.shape[1]
    low_w, lowp = weight_reduce.shape
    nb, ns = lax.axis_size("band"), lax.axis_size("sect")
    nx = ns // 2
    cs = cols // nx
    assert mb == 2 and ns % 2 == 0
    live = rows // LAND_BLOCK * LAND_MOST if rows % LAND_BLOCK == 0 else rows
    off, order = plan(rows, nb)
    n_off = max(len(off), 1)
    n_all = len(off) + 4
    pad = -(-max(DILATIONS) // 8) * 8
    vm, dma = pltpu.VMEM, pltpu.SemaphoreType.DMA
    dims = (mb, rows, cols, ch, br_w, live, nb, ns, low_w, lowp)
    scratch = [
        vm(features.shape, BF16),
        vm(low_level.shape, BF16),
        vm((2, mb, cols, low_w), BF16),
        vm(weight_one.shape, BF16),
        vm((3 + len(off), 3, ch, br_w), BF16),
        vm(weight_pool.shape, BF16),
        vm(weight_project.shape, BF16),
        vm(weight_merging.shape, BF16),
        vm((mb, live, cols, ch), BF16),
        vm((rows, cols + 2 * pad, br_w), F32),
        vm((rows, cols + 2 * pad, br_w), F32),
        vm((n_off, 2, rows, cols, br_w), BF16),
        vm((n_off, rows, cols, br_w), BF16),
        vm((n_off, nx, rows, cs, br_w), BF16),
        vm((n_off, nx, rows, cs, br_w), BF16),
        vm((n_off, rows, cs, br_w), BF16),
        vm((n_off, rows, cs, br_w), BF16),
        vm((4, 2, live, cols, br_w), BF16),
        vm((4, live, cols, br_w), BF16),
        vm((4, nx, live, cs, br_w), BF16),
        vm((4, nx, live, cs, br_w), BF16),
        vm((n_off, rows, cs, br_w), F32),
        vm((4, live, cs, br_w), F32),
        vm((8, ch), F32),
        vm((ns, 8, br_w), F32),
        vm((nb, 8, br_w), F32),
        vm((ns, live, cs, br_w), BF16),
        vm((2, ns, cs, br_w), BF16),
        vm((mb, rows + 2, cols, br_w), BF16),
        vm((mb, rows + 2, cols, lowp), BF16),
        vm((mb, live, cols, br_w), F32),
        vm((live, cols, br_w), F32),
        dma((10 + len(off),)),
        dma((2,)),
        dma((2,)),
        dma((n_all,)),
        dma((n_all,)),
        dma((n_all, nx)),
        dma((n_all, nx)),
        dma((n_off,)),
        dma((n_off,)),
        dma((ns,)),
        dma((ns,)),
        dma((nb,)),
        dma((nb,)),
        dma((ns,)),
        dma((ns,)),
        dma((2, ns)),
        dma((2, ns)),
    ]
    anym = pl.BlockSpec(memory_space=pl.ANY)
    vmem = pl.BlockSpec(memory_space=pltpu.VMEM)
    smem = pl.BlockSpec(memory_space=pltpu.SMEM)
    return pl.pallas_call(
        functools.partial(kernel, dims),
        out_shape=jax.ShapeDtypeStruct((mb, rows, cols, weight_merging.shape[3]), BF16),
        in_specs=[
            smem, anym, anym, anym, anym, vmem, anym, vmem, anym, vmem, vmem, vmem, anym, vmem,
        ],
        out_specs=vmem,
        scratch_shapes=scratch,
        compiler_params=pltpu.CompilerParams(
            collective_id=0, has_side_effects=True, vmem_limit_bytes=60 * 1024 * 1024
        ),
    )(
        land_mask, features, low_level, weight_one, weight_dilated, bias_branch, weight_pool,
        bias_pool.reshape(1, -1), weight_project, bias_project.reshape(1, -1), weight_reduce,
        bias_reduce.reshape(1, -1), weight_merging, bias_merging.reshape(1, -1),
    )


def solution(mesh):
    in_specs = (
        P("grp", "band", None, "sect"),
        P("grp", "band", None, None),
        P("grp", "band"),
        P("sect", None),
        P(None, None, None, "sect", None),
        P(),
        P("sect", None),
        P(),
        P(),
        P(),
        P(),
        P(),
        P(),
        P(),
    )
    out_specs = P("grp", "band", None, None)
    return jax.shard_map(shards, mesh=mesh, in_specs=in_specs, out_specs=out_specs, check_vma=False)
```

time: 207 us -> 37.2 us (0.18); the launches traced: 204 us -> 36.9 us
  waiting for transfers between devices: 78.3 us -> 0 us
  matrix products: 36.1 us -> 0 us
  Pallas kernels: 0 us -> 33.5 us
  blocking collectives: 26.3 us -> 0 us
  local copies, waits for them, and re-layouts: 25.2 us -> 3.39 us
  starting transfers between devices: 21 us -> 0 us
  between operations: 14 us -> 0.01 us
  other arithmetic: 3.7 us -> 0 us
    ppermute x8 -> x0, waiting for transfers between devices: 62.7 us -> none  [the longest x6 57.1 us: from_behind(): return lax.ppermute(value, axis, pairs)]
    dot_general x42 -> x0, matrix products: 36.1 us -> none  [the longest x27 28.3 us: branch_terms(): jnp.dot(tap_rows, weight_dilated[branch_index, row_tap, col_tap], preferr...]
    pallas_call x0 -> x1, Pallas kernels: none -> 33.5 us  [shards(): pl.pallas_call(functools.partial(kernel, dims), out_shape=jax.ShapeDtypeS...]
    ppermute x8 -> x0, starting transfers between devices: 21 us -> none  [the longest x6 16.6 us: from_behind(): return lax.ppermute(value, axis, pairs)]
    psum x2 -> x0, blocking collectives: 18.4 us -> none  [the longest x1 10.6 us: pool_context(): lax.psum(jnp.dot(average, weight_full, precision=PRECISE), 'sect')]
    reduce_scatter x1 -> x0, waiting for transfers between devices: 15.6 us -> none  [shards(): lax.psum_scatter(flat_terms, 'sect', scatter_dimension=0, tiled=True)]
    slice x2 -> x0, local copies, waits for them, and re-layouts: 13.1 us -> none  [the longest x1 12.3 us: branch_terms(): tap_rows = band_rows[:, :, left:left + col_count].reshape(-1, channels)]
    unnamed x69 -> x2, local copies, waits for them, and re-layouts: 11.7 us -> 3.39 us
  transfers between devices with their start and end apart: 9 -> 0, of which waited for: 8 -> 0; matrix products, arithmetic and copies ran while one was open for 10% -> 0% of each run, Pallas kernels for 0% -> 0%
where the time goes in v1:
time: 37.2 us; the launch traced here: 36.9 us
  Pallas kernels  33.5 us (90%)
  local copies, waits for them, and re-layouts  3.39 us (9%)
    pallas_call x1, Pallas kernels, shards(): pl.pallas_call(functools.partial(kernel, dims), out_shape=jax.ShapeDtypeS...  33.5 us
    unnamed x2, local copies, waits for them, and re-layouts  3.39 us

profile of v1, /device:TPU:1, one launch (start us, length us, event | category | flops | bytes accessed | tf_op | source)
XLA Modules:
  0.0 36.9 jit_solution(2686288614758906581)
XLA Ops:
  0.0 1.5 %copy.15.wr = bf16[256,48]{1,0:T(8,128)(2,1)} copy(bf16[256,48]{0,1:T(8,128)(2,1)} %param.24) | data formatting | bytes 49152 | tf_op args[10]
  1.5 33.5 %shard_map.136 = bf16[2,6,96,256]{3,2,1,0:T(8,128)(2,1)} custom-call(s32[2,6]{1,0:T(2,128)} %mask.1, bf16[2,6,96,512]{3,2,1,0:T(8,128)(2,1)} %feat_h.1, bf16[2,6,96,256]{3,2,1,0:T(8,128)(2,1)} %low_h.1, bf16[512,256]{1,0:T(8,128)(2,1)} %w1_h.1, bf16[3,3,3,512,256]{4,3,2,1,0:T(8,128)(2,1)} %wd_h.1, f32[4,256]{1,0:T(4,128)} %bbr.1, bf16[512,256]{1,0:T(8,128)(2,1)} %wpool_h.1, ...), custom_call_target="tpu_custom_call" | custom-call | tf_op jit(solution)/shard_map/pallas_call | solution.py:540
  35.0 1.9 %copy.17 = bf16[2,6,96,256]{3,2,1,0:T(8,128)(2,1)} copy(bf16[2,6,96,256]{3,2,1,0:T(8,128)(2,1)} %shard_map.136) | data formatting | bytes 1179648

commit v2 on v1

--- a/solution.py
+++ b/solution.py
@@ -25,19 +25,19 @@
         if hop < bands:
             off.append((k, 0, hop))
             off.append((k, 2, hop))
-    order = [k for k in (3, 2, 1, 0)]
+    order = [3, 2, 0, 1]
     return off, order
 
 
 def kernel(
     dims, mask, feat_h, low_h, w1_h, wd_h, bbr, wpool_h, bpool, wproj_h, bproj, wr, br, wm_h, bm,
     out,
-    feat, low, low_halo, w1, wd, wpool, wproj, wm, comp, m_l, m_r,
+    feat, low, low_halo, w1, wd, wpool, wproj, wmp, wml, comp, m_l, m_r,
     part_off, crecv_off, xsend_off, xrecv_off, zsend, zrecv,
     part_own, crecv_own, xsend_own, xrecv_own, keep_off, keep_own,
-    sums, pool_s, pool_b, gath, halo, joined, lowred, lowacc, outc,
+    sums, pool_s, pool_b, gath, gath_b, halo, joined, lowred, lowacc, outc,
     loc_sem, lo_s, lo_r, c_s, c_r, x_s, x_r, z_s, z_r, ps_s, ps_r, pb_s, pb_r,
-    g_s, g_r, h_s, h_r,
+    gx_s, gx_r, gc_s, gc_r, hx_s, hx_r, hc_s, hc_r,
 ):
     mb, rows, cols, ch, br_w, live, nb, ns, low_w, lowp = dims
     nx = ns // 2
@@ -70,7 +70,10 @@
     fetch("wpool", wpool_h, wpool)
     fetch("low", low_h, low)
     fetch("wproj", wproj_h, wproj)
-    fetch("wm", wm_h, wm)
+    fetch("wml", wm_h.at[:, :, pl.ds(br_w, lowp)], wml)
+    for i in range(3):
+        for j in range(3):
+            fetch(("wmp", i, j), wm_h.at[i, j, pl.ds(0, br_w)], wmp.at[j, pl.ds(i * br_w, br_w)])
 
     bar = pltpu.get_barrier_semaphore()
     up_ok = band >= 1
@@ -86,11 +89,8 @@
     for ok, step in ((up_ok, -1), (dn_ok, 1)):
         @pl.when(ok)
         def _(step=step):
-            for e in range(1, ns):
-                hello(band + step, lax.rem(sect + e, ns))
-    sides_held = jnp.minimum(band, 1) + jnp.minimum(nb - 1 - band, 1)
-    pl.semaphore_wait(bar, (ns - 1) + (nb - 1) + (ns - 1) * sides_held)
-
+            for e in range(1, nx):
+                hello(band + step, lax.rem(sect + 2 * e, ns))
     def rcopy(src, dst, s, r, **where):
         return pltpu.make_async_remote_copy(
             src_ref=src, dst_ref=dst, send_sem=s, recv_sem=r, device_id=where, device_id_type=MESH
@@ -100,14 +100,6 @@
     low_dn = rcopy(
         low_h.at[:, rows - 1], low_halo.at[0], lo_s.at[1], lo_r.at[0], band=band + 1, sect=sect
     )
-
-    @pl.when(up_ok)
-    def _():
-        low_up.start()
-
-    @pl.when(dn_ok)
-    def _():
-        low_dn.start()
 
     def slots(m):
         on = [mask[m, y] for y in range(rows)]
@@ -131,6 +123,8 @@
         zero = jnp.zeros((ref.shape[0], pad, br_w), F32)
         ref[:, :pad] = zero
         ref[:, pad + cols :] = zero
+    for at in (0, rows + 1):
+        joined[:, at] = jnp.zeros((mb, cols, br_w), BF16)
 
     locals_["feat"].wait()
 
@@ -181,9 +175,10 @@
                     )
                 part_own[t - n_off, step] = val.astype(BF16)
 
-            @pl.when(step == 0)
-            def _():
-                core_copy(t).start()
+            if t >= n_off:
+                @pl.when(step == 0)
+                def _():
+                    core_copy(t).start()
             return carry
 
         lax.fori_loop(0, 2, body, 0)
@@ -243,6 +238,19 @@
     for t in range(n_off):
         locals_[off[t][:2]].wait()
         guarded(first, t)
+
+    sides_held = jnp.minimum(band, 1) + jnp.minimum(nb - 1 - band, 1)
+    pl.semaphore_wait(bar, (ns - 1) + (nb - 1) + (nx - 1) * sides_held)
+
+    for t in range(n_off):
+        guarded(lambda t: core_copy(t).start(), t)
+    @pl.when(up_ok)
+    def _():
+        low_up.start()
+
+    @pl.when(dn_ok)
+    def _():
+        low_dn.start()
 
     facts = [slots(m) for m in range(mb)]
     sums[...] = jnp.zeros_like(sums)
@@ -305,11 +313,14 @@
     second(t0 + 3)
 
     locals_["low"].wait()
-    locals_["wm"].wait()
+    locals_["wml"].wait()
 
     def reduced(v):
         return jax.nn.relu(
-            jnp.dot(v, wr[...], preferred_element_type=F32) + br[...]
+            lax.dot_general(
+                v, wr[...], (((1,), (1,)), ((), ())), preferred_element_type=F32
+            )
+            + br[...]
         ).astype(BF16)
 
     for m in range(mb):
@@ -328,26 +339,24 @@
             for m in range(mb):
                 lowred[m, at] = jnp.zeros((cols, lowp), BF16)
 
-    def merged(source, m, lo, n):
+    def stash(terms):
+        for ref, term in zip((m_l, m_r), (terms[0], terms[2])):
+            ref[:live, pl.ds(pad, cols)] = term.reshape(live, cols, br_w)
+        outc[...] = terms[1].reshape(live, cols, br_w)
+
+    def combined():
+        return outc[...] + m_l[:live, pl.ds(pad - 1, cols)] + m_r[:live, pl.ds(pad + 1, cols)]
+
+    for m in range(mb):
         row_of = facts[m][2]
-        sides = [None] * 3
+        terms = [None] * 3
         for i in range(3):
-            lhs = jnp.concatenate([source[m, row_of[r] + i] for r in range(live)], axis=0)
+            lhs = jnp.concatenate([lowred[m, row_of[r] + i] for r in range(live)], axis=0)
             for j in range(3):
-                term = jnp.dot(
-                    lhs, wm[i, j, lo : lo + n], preferred_element_type=F32
-                )
-                sides[j] = term if sides[j] is None else sides[j] + term
-        m_l[:live, pl.ds(pad, cols)] = sides[0].reshape(live, cols, br_w)
-        m_r[:live, pl.ds(pad, cols)] = sides[2].reshape(live, cols, br_w)
-        return (
-            sides[1].reshape(live, cols, br_w)
-            + m_l[:live, pl.ds(pad - 1, cols)]
-            + m_r[:live, pl.ds(pad + 1, cols)]
-        )
-
-    for m in range(mb):
-        lowacc[m] = merged(lowred, m, br_w, lowp) + bm[...].reshape(1, 1, br_w)
+                term = jnp.dot(lhs, wml[i, j], preferred_element_type=F32)
+                terms[j] = term if i == 0 else terms[j] + term
+        stash(terms)
+        lowacc[m] = combined() + bm[...].reshape(1, 1, br_w)
 
     locals_["wproj"].wait()
     for e in range(1, nb):
@@ -382,57 +391,91 @@
         )
     done = jax.nn.relu(acc + base).reshape(live, cs, br_w)
     for r in range(live):
-        gath[sect, r] = (done[r] * own_held[r].astype(F32)).astype(BF16)
-
-    def gather_copy(e, incoming=False):
-        other = lax.rem(sect + e, ns)
-        slot = other if incoming else sect
-        return rcopy(gath.at[sect], gath.at[slot], g_s.at[other], g_r.at[slot], sect=other)
-
-    def halo_copy(side, e, incoming=False):
-        other = lax.rem(sect + e, ns)
-        slot = other if incoming else sect
-        src = gath.at[sect, live - 1 if side == 0 else 0]
+        gath[xi, r] = (done[r] * own_held[r].astype(F32)).astype(BF16)
+
+    peer = xi * 2 + 1 - core
+
+    def gather_x(e, incoming=False):
+        other = lax.rem(xi + e, nx)
+        slot = other if incoming else xi
         return rcopy(
-            src, halo.at[side, slot], h_s.at[side, other], h_r.at[side, slot],
-            band=band + 1 if side == 0 else band - 1, sect=other,
-        )
-
-    for e in range(1, ns):
-        gather_copy(e).start()
+            gath.at[xi], gath.at[slot], gx_s.at[other], gx_r.at[slot], sect=other * 2 + core
+        )
+
+    def gather_core(c):
+        return rcopy(gath.at[c], gath_b.at[c], gc_s.at[c], gc_r.at[c], sect=peer)
+
+    def halo_x(side, e, incoming=False):
+        other = lax.rem(xi + e, nx)
+        slot = other if incoming else xi
+        src = gath.at[xi, live - 1 if side == 0 else 0]
+        return rcopy(
+            src, halo.at[side, slot * 2 + core], hx_s.at[side, other], hx_r.at[side, slot],
+            band=band + 1 if side == 0 else band - 1, sect=other * 2 + core,
+        )
+
+    def halo_core(side, c, incoming=False):
+        cell = c * 2 + (1 - core if incoming else core)
+        return rcopy(
+            halo.at[side, cell], halo.at[side, cell], hc_s.at[side, c], hc_r.at[side, c], sect=peer
+        )
+
+    for e in range(1, nx):
+        gather_x(e).start()
     for side, ok in ((0, dn_ok), (1, up_ok)):
         @pl.when(ok)
         def _(side=side):
-            for e in range(ns):
-                halo_copy(side, e).start()
-    for e in range(1, ns):
-        gather_copy(e, True).wait_recv()
-    for m in range(mb):
-        on, slot_of, _, _ = facts[m]
+            for e in range(nx):
+                halo_x(side, e).start()
+    gather_core(xi).start()
+    for i in range(3):
+        for j in range(3):
+            locals_[("wmp", i, j)].wait()
+    for e in range(1, nx):
+        gather_x(e, True).wait_recv()
+        gather_core(lax.rem(xi + e, nx)).start()
+
+    for step in range(2):
+        image = core if step == 0 else 1 - core
+        on, slot_of, row_of, _ = slots(image)
+        cells = gath if step == 0 else gath_b
+        if step == 1:
+            for c in range(nx):
+                gather_core(c).wait_recv()
         for y in range(rows):
             for c in range(nx):
-                joined[m, y + 1, pl.ds(c * cs, cs)] = (
-                    gath[c * 2 + m, slot_of[y]].astype(F32) * on[y].astype(F32)
+                joined[image, y + 1, pl.ds(c * cs, cs)] = (
+                    cells[c, slot_of[y]].astype(F32) * on[y].astype(F32)
                 ).astype(BF16)
-    for side, at, ok in ((0, 0, up_ok), (1, rows + 1, dn_ok)):
-        @pl.when(ok)
-        def _(side=side, at=at):
-            for e in range(ns):
-                halo_copy(side, e, True).wait_recv()
-            for m in range(mb):
-                for c in range(nx):
-                    joined[m, at, pl.ds(c * cs, cs)] = halo[side, c * 2 + m]
-
-        @pl.when(jnp.logical_not(ok))
-        def _(at=at):
-            for m in range(mb):
-                joined[m, at] = jnp.zeros((cols, br_w), BF16)
-
-    for m in range(mb):
-        on, slot_of, _, _ = facts[m]
-        outc[...] = jax.nn.relu(merged(joined, m, 0, br_w) + lowacc[m])
+        lhs = jnp.concatenate(
+            [
+                jnp.concatenate([joined[image, row_of[r] + i] for r in range(live)], axis=0)
+                for i in range(3)
+            ],
+            axis=1,
+        )
+        stash([jnp.dot(lhs, wmp[j], preferred_element_type=F32) for j in range(3)])
+        for side, ok in ((0, up_ok), (1, dn_ok)):
+            @pl.when(ok)
+            def _(side=side, step=step, image=image):
+                for e in range(nx):
+                    if step == 0:
+                        halo_x(side, e, True).wait_recv()
+                        halo_core(side, lax.rem(xi + e, nx)).start()
+                    else:
+                        halo_core(side, e, True).wait_recv()
+                edge = jnp.concatenate([halo[side, c * 2 + image] for c in range(nx)], axis=0)
+                at = 0 if side == 0 else live - 1
+                tap = pl.ds(2 * br_w * side, br_w)
+                add = [
+                    jnp.dot(edge, wmp[j, tap], preferred_element_type=F32) for j in range(3)
+                ]
+                m_l[at, pl.ds(pad, cols)] = m_l[at, pl.ds(pad, cols)] + add[0]
+                outc[at] = outc[at] + add[1]
+                m_r[at, pl.ds(pad, cols)] = m_r[at, pl.ds(pad, cols)] + add[2]
+        outc[...] = jax.nn.relu(combined() + lowacc[image])
         for y in range(rows):
-            out[m, y] = (outc[slot_of[y]] * on[y].astype(F32)).astype(BF16)
+            out[image, y] = outc[slot_of[y]].astype(BF16)
 
     @pl.when(up_ok)
     def _():
@@ -454,14 +497,22 @@
         left(t0 + u)
     for e in range(1, ns):
         pool_sect(e).wait_send()
-        gather_copy(e).wait_send()
     for e in range(1, nb):
         pool_band(e).wait_send()
+    for e in range(1, nx):
+        gather_x(e).wait_send()
+    for c in range(nx):
+        gather_core(c).wait_send()
     for side, ok in ((0, dn_ok), (1, up_ok)):
         @pl.when(ok)
         def _(side=side):
-            for e in range(ns):
-                halo_copy(side, e).wait_send()
+            for e in range(nx):
+                halo_x(side, e).wait_send()
+    for side, ok in ((0, up_ok), (1, dn_ok)):
+        @pl.when(ok)
+        def _(side=side):
+            for c in range(nx):
+                halo_core(side, c).wait_send()
 
 
 def shards(
@@ -491,7 +542,8 @@
         vm((3 + len(off), 3, ch, br_w), BF16),
         vm(weight_pool.shape, BF16),
         vm(weight_project.shape, BF16),
-        vm(weight_merging.shape, BF16),
+        vm((3, 3 * br_w, weight_merging.shape[3]), BF16),
+        vm((3, 3, lowp, weight_merging.shape[3]), BF16),
         vm((mb, live, cols, ch), BF16),
         vm((rows, cols + 2 * pad, br_w), F32),
         vm((rows, cols + 2 * pad, br_w), F32),
@@ -510,13 +562,14 @@
         vm((8, ch), F32),
         vm((ns, 8, br_w), F32),
         vm((nb, 8, br_w), F32),
-        vm((ns, live, cs, br_w), BF16),
+        vm((nx, live, cs, br_w), BF16),
+        vm((nx, live, cs, br_w), BF16),
         vm((2, ns, cs, br_w), BF16),
         vm((mb, rows + 2, cols, br_w), BF16),
         vm((mb, rows + 2, cols, lowp), BF16),
         vm((mb, live, cols, br_w), F32),
         vm((live, cols, br_w), F32),
-        dma((10 + len(off),)),
+        dma((19 + len(off),)),
         dma((2,)),
         dma((2,)),
         dma((n_all,)),
@@ -529,15 +582,19 @@
         dma((ns,)),
         dma((nb,)),
         dma((nb,)),
-        dma((ns,)),
-        dma((ns,)),
-        dma((2, ns)),
-        dma((2, ns)),
+        dma((nx,)),
+        dma((nx,)),
+        dma((nx,)),
+        dma((nx,)),
+        dma((2, nx)),
+        dma((2, nx)),
+        dma((2, nx)),
+        dma((2, nx)),
     ]
     anym = pl.BlockSpec(memory_space=pl.ANY)
     vmem = pl.BlockSpec(memory_space=pltpu.VMEM)
     smem = pl.BlockSpec(memory_space=pltpu.SMEM)
-    return pl.pallas_call(
+    merged_map = pl.pallas_call(
         functools.partial(kernel, dims),
         out_shape=jax.ShapeDtypeStruct((mb, rows, cols, weight_merging.shape[3]), BF16),
         in_specs=[
@@ -550,9 +607,10 @@
         ),
     )(
         land_mask, features, low_level, weight_one, weight_dilated, bias_branch, weight_pool,
-        bias_pool.reshape(1, -1), weight_project, bias_project.reshape(1, -1), weight_reduce,
+        bias_pool.reshape(1, -1), weight_project, bias_project.reshape(1, -1), weight_reduce.T,
         bias_reduce.reshape(1, -1), weight_merging, bias_merging.reshape(1, -1),
     )
+    return jnp.where(land_mask[:, :, None, None] != 0, merged_map, jnp.zeros_like(merged_map))
 
 
 def solution(mesh):

time: 37.2 us -> 34.1 us (0.917)
  local copies, waits for them, and re-layouts: 3.39 us -> 0 us
  other arithmetic: 0 us -> 2.67 us
  Pallas kernels: 33.5 us -> 30.9 us
    unnamed x2 -> x0, local copies, waits for them, and re-layouts: 3.39 us -> none
    pallas_call x1, Pallas kernels: 33.5 us -> 30.9 us  [shards(): pl.pallas_call(functools.partial(kernel, dims), out_shape=jax.ShapeDtypeS...]
    select_n x0 -> x1, other arithmetic: none -> 1.99 us  [shards(): jnp.where(land_mask[:, :, None, None] != 0, merged_map, jnp.zeros_like(me...]
    ne x0 -> x1, other arithmetic: none -> 0.68 us  [shards(): land_mask[:, :, None, None] != 0]
where the time goes in v2:
time: 34.1 us; the launch traced here: 33.6 us
  Pallas kernels  30.9 us (91%)
  other arithmetic  2.67 us (8%)
    pallas_call x1, Pallas kernels, shards(): pl.pallas_call(functools.partial(kernel, dims), out_shape=jax.ShapeDtypeS...  30.9 us
    select_n x1, other arithmetic, shards(): jnp.where(land_mask[:, :, None, None] != 0, merged_map, jnp.zeros_like(me...  1.99 us
    ne x1, other arithmetic, shards(): land_mask[:, :, None, None] != 0  0.68 us

profile of v2, /device:TPU:1, one launch (start us, length us, event | category | flops | bytes accessed | tf_op | source)
XLA Modules:
  0.0 33.6 jit_solution(10480566542941753258)
XLA Ops:
  0.0 0.7 %broadcast_compare_fusion = pred[2,6]{1,0:T(4,128)(4,1)S(1)} fusion(s32[2,6]{1,0:T(2,128)} %mask.1), kind=kLoop, calls=%fused_computation.1 | loop fusion | flops 12 | bytes 60 | tf_op jit(solution)/shard_map/ne | solution.py:613
  0.7 30.9 %shard_map.136 = bf16[2,6,96,256]{3,2,1,0:T(8,128)(2,1)} custom-call(s32[2,6]{1,0:T(2,128)} %mask.1, bf16[2,6,96,512]{3,2,1,0:T(8,128)(2,1)} %feat_h.1, bf16[2,6,96,256]{3,2,1,0:T(8,128)(2,1)} %low_h.1, bf16[512,256]{1,0:T(8,128)(2,1)} %w1_h.1, bf16[3,3,3,512,256]{4,3,2,1,0:T(8,128)(2,1)} %wd_h.1, f32[4,256]{1,0:T(4,128)} %bbr.1, bf16[512,256]{1,0:T(8,128)(2,1)} %wpool_h.1, ...), custom_call_target="tpu_custom_call" | custom-call | tf_op jit(solution)/shard_map/pallas_call | solution.py:597
  31.6 2.0 %broadcast_select_fusion = bf16[2,6,96,256]{3,2,1,0:T(8,128)(2,1)} fusion(bf16[2,6,96,256]{3,2,1,0:T(8,128)(2,1)} %shard_map.136, pred[2,6]{1,0:T(4,128)(4,1)S(1)} %broadcast_compare_fusion), kind=kLoop, calls=%fused_computation | loop fusion | flops 294912 | bytes 1179660 | tf_op jit(solution)/shard_map/jit(_where)/select_n | solution.py:613

commit v3 on v2

--- a/solution.py
+++ b/solution.py
@@ -62,12 +62,12 @@
     fetch("feat", feat_h, feat)
     for k, i, _ in off:
         fetch((k, i), wd_h.at[k - 1, i], wd.at[need.index((k, i))])
+    fetch("wpool", wpool_h, wpool)
     for k in order:
         if k:
             fetch((k, 1), wd_h.at[k - 1, 1], wd.at[need.index((k, 1))])
         else:
             fetch("w1", w1_h, w1)
-    fetch("wpool", wpool_h, wpool)
     fetch("low", low_h, low)
     fetch("wproj", wproj_h, wproj)
     fetch("wml", wm_h.at[:, :, pl.ds(br_w, lowp)], wml)
@@ -252,18 +252,7 @@
     def _():
         low_dn.start()
 
-    facts = [slots(m) for m in range(mb)]
     sums[...] = jnp.zeros_like(sums)
-    for m in range(mb):
-        for r in range(live):
-            comp[m, r] = feat[m, facts[m][2][r]]
-
-    t0 = n_off
-    locals_[(order[0], 1) if order[0] else "w1"].wait()
-    first(t0)
-    for t in range(n_off):
-        guarded(second, t)
-
     locals_["wpool"].wait()
     for m in range(mb):
         acc = jnp.zeros((cols, ch), F32)
@@ -291,12 +280,23 @@
     for e in range(1, ns):
         pool_sect(e).start()
 
-    locals_[(order[1], 1) if order[1] else "w1"].wait()
-    first(t0 + 1)
+    facts = [slots(m) for m in range(mb)]
+    for m in range(mb):
+        for r in range(live):
+            comp[m, r] = feat[m, facts[m][2][r]]
+
+    for t in range(n_off):
+        guarded(second, t)
+
+    t0 = n_off
+
+    def own(u):
+        locals_[(order[u], 1) if order[u] else "w1"].wait()
+        first(t0 + u)
+
+    own(0)
+    own(1)
     second(t0)
-    for t in range(n_off):
-        guarded(third_off, t)
-
     for e in range(1, ns):
         pool_sect(e, True).wait_recv()
     total = pool_s[0]
@@ -306,10 +306,12 @@
     for e in range(1, nb):
         pool_band(e).start()
 
-    for u in (2, 3):
-        locals_[(order[u], 1) if order[u] else "w1"].wait()
-        first(t0 + u)
-        second(t0 + u - 1)
+    own(2)
+    second(t0 + 1)
+    own(3)
+    second(t0 + 2)
+    for t in range(n_off):
+        guarded(third_off, t)
     second(t0 + 3)
 
     locals_["low"].wait()

time: 34.1 us -> 33.2 us (0.974)
  Pallas kernels: 30.9 us -> 29.9 us
    pallas_call x1, Pallas kernels: 30.9 us -> 29.9 us  [shards(): pl.pallas_call(functools.partial(kernel, dims), out_shape=jax.ShapeDtypeS...]
where the time goes in v3:
time: 33.2 us; the launch traced here: 32.6 us
  Pallas kernels  29.9 us (90%)
  other arithmetic  2.67 us (8%)
    pallas_call x1, Pallas kernels, shards(): pl.pallas_call(functools.partial(kernel, dims), out_shape=jax.ShapeDtypeS...  29.9 us
    select_n x1, other arithmetic, shards(): jnp.where(land_mask[:, :, None, None] != 0, merged_map, jnp.zeros_like(me...  1.99 us
    ne x1, other arithmetic, shards(): land_mask[:, :, None, None] != 0  0.68 us

profile of v3, /device:TPU:1, one launch (start us, length us, event | category | flops | bytes accessed | tf_op | source)
XLA Modules:
  0.0 32.6 jit_solution(17045867777041500432)
XLA Ops:
  0.0 0.7 %broadcast_compare_fusion = pred[2,6]{1,0:T(4,128)(4,1)S(1)} fusion(s32[2,6]{1,0:T(2,128)} %mask.1), kind=kLoop, calls=%fused_computation.1 | loop fusion | flops 12 | bytes 60 | tf_op jit(solution)/shard_map/ne | solution.py:615
  0.7 29.9 %shard_map.136 = bf16[2,6,96,256]{3,2,1,0:T(8,128)(2,1)} custom-call(s32[2,6]{1,0:T(2,128)} %mask.1, bf16[2,6,96,512]{3,2,1,0:T(8,128)(2,1)} %feat_h.1, bf16[2,6,96,256]{3,2,1,0:T(8,128)(2,1)} %low_h.1, bf16[512,256]{1,0:T(8,128)(2,1)} %w1_h.1, bf16[3,3,3,512,256]{4,3,2,1,0:T(8,128)(2,1)} %wd_h.1, f32[4,256]{1,0:T(4,128)} %bbr.1, bf16[512,256]{1,0:T(8,128)(2,1)} %wpool_h.1, ...), custom_call_target="tpu_custom_call" | custom-call | tf_op jit(solution)/shard_map/pallas_call | solution.py:599
  30.6 2.0 %broadcast_select_fusion = bf16[2,6,96,256]{3,2,1,0:T(8,128)(2,1)} fusion(bf16[2,6,96,256]{3,2,1,0:T(8,128)(2,1)} %shard_map.136, pred[2,6]{1,0:T(4,128)(4,1)S(1)} %broadcast_compare_fusion), kind=kLoop, calls=%fused_computation | loop fusion | flops 294912 | bytes 1179660 | tf_op jit(solution)/shard_map/jit(_where)/select_n | solution.py:615

commit v4 on v3

--- a/solution.py
+++ b/solution.py
@@ -35,8 +35,8 @@
     feat, low, low_halo, w1, wd, wpool, wproj, wmp, wml, comp, m_l, m_r,
     part_off, crecv_off, xsend_off, xrecv_off, zsend, zrecv,
     part_own, crecv_own, xsend_own, xrecv_own, keep_off, keep_own,
-    sums, pool_s, pool_b, gath, gath_b, halo, joined, lowred, lowacc, outc,
-    loc_sem, lo_s, lo_r, c_s, c_r, x_s, x_r, z_s, z_r, ps_s, ps_r, pb_s, pb_r,
+    sel, sel_got, sums, pool_s, pool_b, gath, gath_b, halo, joined, lowred, lowacc, outc,
+    loc_sem, se_s, se_r, lo_s, lo_r, c_s, c_r, x_s, x_r, z_s, z_r, ps_s, ps_r, pb_s, pb_r,
     gx_s, gx_r, gc_s, gc_r, hx_s, hx_r, hc_s, hc_r,
 ):
     mb, rows, cols, ch, br_w, live, nb, ns, low_w, lowp = dims
@@ -125,6 +125,14 @@
         ref[:, pad + cols :] = zero
     for at in (0, rows + 1):
         joined[:, at] = jnp.zeros((mb, cols, br_w), BF16)
+
+    _, _, own_row, own_held = slots(core)
+    sel[...] = jnp.zeros_like(sel)
+    for r in range(1, live - 1):
+        for y in range(1, rows - 1):
+            sel[r, pl.ds(y, 1)] = jnp.where(
+                own_row[r] == y, jnp.ones((1, br_w), F32), jnp.zeros((1, br_w), F32)
+            )
 
     locals_["feat"].wait()
 
@@ -185,6 +193,8 @@
 
     def second(t):
         core_copy(t).wait_recv()
+        if t < n_off:
+            sel_copy(t).wait_recv()
         part, got, send, keep, u = (
             (part_off, crecv_off, xsend_off, keep_off, t)
             if t < n_off
@@ -193,6 +203,14 @@
         for c in range(nx):
             cell = pl.ds(c * cs, cs)
             total = part[u, 1, :, cell].astype(F32) + got[u, :, cell].astype(F32)
+            if t < n_off:
+                kept = [total[0]]
+                for r in range(1, live - 1):
+                    row = jnp.zeros((cs, br_w), F32)
+                    for y in range(1, rows - 1):
+                        row = row + sel_got[u, r, pl.ds(y, 1)] * total[y]
+                    kept.append(row)
+                total = jnp.stack(kept + [total[rows - 1]], axis=0)
             send[u, c] = total.astype(BF16)
 
             @pl.when(xi == c)
@@ -226,6 +244,13 @@
             band=band + hop if i == 0 else band - hop, sect=sect,
         )
 
+    def sel_copy(t):
+        k, i, hop = off[t]
+        return rcopy(
+            sel, sel_got.at[t], se_s.at[t], se_r.at[t],
+            band=band - hop if i == 0 else band + hop, sect=sect,
+        )
+
     def third_off(t):
         zsend[t] = shared(t).astype(BF16)
         z_copy(t).start()
@@ -244,6 +269,10 @@
 
     for t in range(n_off):
         guarded(lambda t: core_copy(t).start(), t)
+    for t in range(n_off):
+        @pl.when(gets_from(t))
+        def _(t=t):
+            sel_copy(t).start()
     @pl.when(up_ok)
     def _():
         low_up.start()
@@ -375,7 +404,6 @@
         mine = jnp.where(core == m, context[m : m + 1], mine)
     base = mine + bproj[...]
 
-    _, _, own_row, own_held = slots(core)
     acc = jnp.zeros((live * cs, br_w), F32)
     for u, k in enumerate(order):
         keep_own[u] = shared(t0 + u)
@@ -384,8 +412,7 @@
                 @pl.when(gets_from(t))
                 def _(t=t, u=u):
                     z_copy(t).wait_recv()
-                    for r in range(live):
-                        keep_own[u, r] = keep_own[u, r] + zrecv[t, own_row[r]].astype(F32)
+                    keep_own[u] = keep_own[u] + zrecv[t].astype(F32)
         branch = jax.nn.relu(keep_own[u] + bbr[k : k + 1].reshape(1, 1, br_w)).astype(BF16)
         acc = acc + jnp.dot(
             branch.reshape(live * cs, br_w), wproj[k * br_w : (k + 1) * br_w],
@@ -493,6 +520,10 @@
             x_copy(t, e).wait_send()
 
     for t in range(n_off):
+        @pl.when(gets_from(t))
+        def _(t=t):
+            sel_copy(t).wait_send()
+
         guarded(left, t)
         guarded(lambda t: z_copy(t).wait_send(), t)
     for u in range(4):
@@ -551,16 +582,18 @@
         vm((rows, cols + 2 * pad, br_w), F32),
         vm((n_off, 2, rows, cols, br_w), BF16),
         vm((n_off, rows, cols, br_w), BF16),
-        vm((n_off, nx, rows, cs, br_w), BF16),
-        vm((n_off, nx, rows, cs, br_w), BF16),
-        vm((n_off, rows, cs, br_w), BF16),
-        vm((n_off, rows, cs, br_w), BF16),
+        vm((n_off, nx, live, cs, br_w), BF16),
+        vm((n_off, nx, live, cs, br_w), BF16),
+        vm((n_off, live, cs, br_w), BF16),
+        vm((n_off, live, cs, br_w), BF16),
         vm((4, 2, live, cols, br_w), BF16),
         vm((4, live, cols, br_w), BF16),
         vm((4, nx, live, cs, br_w), BF16),
         vm((4, nx, live, cs, br_w), BF16),
-        vm((n_off, rows, cs, br_w), F32),
+        vm((n_off, live, cs, br_w), F32),
         vm((4, live, cs, br_w), F32),
+        vm((live, rows, br_w), F32),
+        vm((n_off, live, rows, br_w), F32),
         vm((8, ch), F32),
         vm((ns, 8, br_w), F32),
         vm((nb, 8, br_w), F32),
@@ -572,6 +605,8 @@
         vm((mb, live, cols, br_w), F32),
         vm((live, cols, br_w), F32),
         dma((19 + len(off),)),
+        dma((n_off,)),
+        dma((n_off,)),
         dma((2,)),
         dma((2,)),
         dma((n_all,)),

time: 33.2 us -> 34.2 us (1.030)
  Pallas kernels: 29.9 us -> 30.9 us
    pallas_call x1, Pallas kernels: 29.9 us -> 30.9 us  [shards(): pl.pallas_call(functools.partial(kernel, dims), out_shape=jax.ShapeDtypeS...]
where the time goes in v4:
time: 34.2 us; the launch traced here: 33.6 us
  Pallas kernels  30.9 us (90%)
  other arithmetic  2.67 us (8%)
    pallas_call x1, Pallas kernels, shards(): pl.pallas_call(functools.partial(kernel, dims), out_shape=jax.ShapeDtypeS...  30.9 us
    select_n x1, other arithmetic, shards(): jnp.where(land_mask[:, :, None, None] != 0, merged_map, jnp.zeros_like(me...  1.99 us

profile of v4, /device:TPU:1, one launch (start us, length us, event | category | flops | bytes accessed | tf_op | source)
XLA Modules:
  0.0 33.6 jit_solution(858288967909265986)
XLA Ops:
  0.0 0.7 %broadcast_compare_fusion = pred[2,6]{1,0:T(4,128)(4,1)S(1)} fusion(s32[2,6]{1,0:T(2,128)} %mask.1), kind=kLoop, calls=%fused_computation.1 | loop fusion | flops 12 | bytes 60 | tf_op jit(solution)/shard_map/ne | solution.py:650
  0.7 30.9 %shard_map.136 = bf16[2,6,96,256]{3,2,1,0:T(8,128)(2,1)} custom-call(s32[2,6]{1,0:T(2,128)} %mask.1, bf16[2,6,96,512]{3,2,1,0:T(8,128)(2,1)} %feat_h.1, bf16[2,6,96,256]{3,2,1,0:T(8,128)(2,1)} %low_h.1, bf16[512,256]{1,0:T(8,128)(2,1)} %w1_h.1, bf16[3,3,3,512,256]{4,3,2,1,0:T(8,128)(2,1)} %wd_h.1, f32[4,256]{1,0:T(4,128)} %bbr.1, bf16[512,256]{1,0:T(8,128)(2,1)} %wpool_h.1, ...), custom_call_target="tpu_custom_call" | custom-call | tf_op jit(solution)/shard_map/pallas_call | solution.py:634
  31.6 2.0 %broadcast_select_fusion = bf16[2,6,96,256]{3,2,1,0:T(8,128)(2,1)} fusion(bf16[2,6,96,256]{3,2,1,0:T(8,128)(2,1)} %shard_map.136, pred[2,6]{1,0:T(4,128)(4,1)S(1)} %broadcast_compare_fusion), kind=kLoop, calls=%fused_computation | loop fusion | flops 294912 | bytes 1179660 | tf_op jit(solution)/shard_map/jit(_where)/select_n | solution.py:650
